TPU v7x, 32 devices: a whole 2x2x4 slice. The times are simulated.
32 devices in a mesh: row: 4 (over x, core), col: 8 (over z, y).
Axes of the slice: x: 2, y: 2, z: 4, core: 2. Of those that a mesh axis runs over, the one named last changes fastest.
Arguments:
- matrix: float32 [24576, 24576], P('row', 'col'), may hold values from -6 to 6
Outputs:
- y_block: float32 [4, 24576], P(None, 'row')
- reflectors: float32 [4, 24576], P(None, 'row')
- t_factor: float32 [4, 4], replicated
All inputs are finite; a program needn't handle non-finite values.
Results may differ from a plain program's by a relative error of at most 0.0003.
Values sent between devices are 32-bit elements; how exact they have to be, the bound alone decides.
A program may use at most 128 MiB of HBM per device.

v0:
```python
import functools

import jax
import jax.numpy as jnp
from jax import lax
from jax.experimental import pallas as pl
from jax.experimental.pallas import tpu as pltpu
from jax.sharding import PartitionSpec as P

K = 4
LANES = 128
MESH = pl.DeviceIdType.MESH
VMEM_BYTES = 67043328
SPARE_BYTES = 5 * 2**19


def plan(R, C, rows, cols):
    q = C // R
    m = cols // LANES
    G = 8 if m % 8 == 0 else m
    ng = m // G
    groups = q * ng
    ring = max(4, q)
    room = (VMEM_BYTES - SPARE_BYTES) // (LANES * cols * 4)
    sp = 0
    while (G - sp) * groups + ring > room:
        sp += 1
    return q, m, G, ng, groups, ring, sp


def lane_total(row):
    return jnp.sum(row, axis=-1, keepdims=True)


def kernel(
    R, C, a_hbm, o_ref, t_ref,
    res, ring, acc, pan, av, xs, pbuf, rbuf, sbuf, rnd, vy, ob, vs, ys, ps,
    res_sem, ring_sem, pan_sem, pan_send, av_sem, p_send, p_recv, s_send, s_recv, o_send, o_recv,
):
    rows, cols = a_hbm.shape
    q, m, G, ng, groups, nring, sp = plan(R, C, rows, cols)
    rp = G - sp
    r = lax.axis_index("row")
    c = lax.axis_index("col")

    def send(src, dst, send_sem, recv_sem, tr, tc):
        same = jnp.logical_and(tr == r, tc == c)

        @pl.when(jnp.logical_not(same))
        def _():
            pltpu.make_async_remote_copy(
                src, dst, send_sem, recv_sem, device_id=(tr, tc), device_id_type=MESH
            ).start()

        @pl.when(same)
        def _():
            pltpu.make_async_copy(src, dst, recv_sem).start()

    def sent(src, dst, send_sem, recv_sem, tr, tc):
        same = jnp.logical_and(tr == r, tc == c)

        @pl.when(jnp.logical_not(same))
        def _():
            pltpu.make_async_remote_copy(
                src, dst, send_sem, recv_sem, device_id=(tr, tc), device_id_type=MESH
            ).wait_send()

    def arrived(ref, sem):
        pltpu.make_async_copy(ref, ref, sem).wait()

    def panel_copy(t):
        return pltpu.make_async_copy(
            a_hbm.at[pl.ds(pl.multiple_of(t * LANES, LANES), LANES), pl.ds(0, LANES)],
            ring.at[lax.div(t, m), :, pl.ds(pl.multiple_of(lax.rem(t, m) * LANES, LANES), LANES)],
            pan_sem,
        )

    @pl.when(c == 0)
    def _():
        @pl.loop(0, q * m)
        def _(t):
            panel_copy(t).start()

    def res_copy(g, i):
        row = pl.multiple_of((g * G + i) * LANES, LANES)
        k = g * rp + i
        return pltpu.make_async_copy(a_hbm.at[pl.ds(row, LANES)], res.at[k], res_sem.at[k])

    def ring_copy(seq):
        n = lax.rem(seq, groups * sp)
        g, u = lax.div(n, sp), lax.rem(n, sp)
        row = pl.multiple_of((g * G + rp + u) * LANES, LANES)
        slot = lax.rem(seq, nring)
        return pltpu.make_async_copy(a_hbm.at[pl.ds(row, LANES)], ring.at[slot], ring_sem.at[slot])

    @pl.loop(0, groups)
    def _(g):
        @pl.loop(0, rp)
        def _(i):
            res_copy(g, i).start()

    barrier = pltpu.get_barrier_semaphore()
    me = r * C + c

    @pl.loop(1, R * C)
    def _(k):
        t = lax.rem(me + k, R * C)
        pl.semaphore_signal(
            barrier, inc=1, device_id=(lax.div(t, C), lax.rem(t, C)), device_id_type=MESH
        )

    def panel_sends(act):
        for part in range(2):
            for piece in range(q):
                for tr in range(R):
                    first, count = (0, 1) if part == 0 else (1, K)
                    act(
                        pan.at[pl.ds(first, count), pl.ds(piece * ng, ng)],
                        av.at[pl.ds(first, count)],
                        pan_send.at[part, piece, tr],
                        av_sem.at[part],
                        jnp.int32(tr),
                        r * q + piece,
                    )

    @pl.when(c == 0)
    def _():
        arrived(ring.at[pl.ds(0, q)], pan_sem)

        @pl.loop(0, groups)
        def _(g):
            slot = lax.div(g, ng)
            for s in range(G):
                at = pl.multiple_of((lax.rem(g, ng) * G + s) * LANES, LANES)
                turned = ring[slot, :, pl.ds(at, LANES)].T
                for k in range(K + 1):
                    pan[k, g, s : s + 1, :] = turned[k : k + 1, :]

    pl.semaphore_wait(barrier, R * C - 1)

    @pl.when(c == 0)
    def _():
        panel_sends(send)

    if sp:
        for seq in range(min(nring, K * groups * sp)):
            ring_copy(jnp.int32(seq)).start()

    sub = lax.broadcasted_iota(jnp.int32, (G, LANES), 0)
    lane = lax.broadcasted_iota(jnp.int32, (G, LANES), 1)
    where_at = [c * cols + (n * G + sub) * LANES + lane for n in range(ng)]
    lane1 = lax.broadcasted_iota(jnp.int32, (1, LANES), 1)
    first_col = (jnp.zeros((1, LANES), jnp.int32) + c) == 0

    def load(ref, *at):
        return [ref[(*at, n)] for n in range(ng)]

    def store(ref, value, *at):
        for n in range(ng):
            ref[(*at, n)] = value[n]

    def pick(row, k):
        return lane_total(jnp.where(lane1 == k, row, 0.0))

    def dots(one, two):
        total = one[0] * two[0]
        for n in range(1, ng):
            total = total + one[n] * two[n]
        return jnp.sum(total, axis=0, keepdims=True)

    def less(value, scale, other):
        return [a - scale * b for a, b in zip(value, other)]

    def round_copy(j, k, o):
        tc = lax.rem(c + o, C)
        return pltpu.make_async_remote_copy(
            sbuf.at[j, k], rnd.at[j, k, c], s_send.at[j, k], s_recv.at[j, k],
            device_id=(r, tc), device_id_type=MESH,
        )

    def round_send(j, k):
        rnd[j, k, c] = sbuf[j, k]

        @pl.loop(1, C)
        def _(o):
            round_copy(j, k, o).start()

    def round_get(j, k):
        arrived(rnd.at[j, k, pl.ds(0, C - 1)], s_recv.at[j, k])
        total = rnd[j, k, 0]
        for n in range(1, C):
            total = total + rnd[j, k, n]
        return total

    def p_targets(j, g, act):
        piece, part = lax.div(g, ng), lax.rem(g, ng)
        for tr in range(R):
            act(
                pbuf.at[j, g], rbuf.at[j, c, part], p_send.at[j, g, tr], p_recv.at[j],
                jnp.int32(tr), r * q + piece,
            )

    def o_targets(j, act):
        for u in range(q):
            act(
                vy.at[j], ob.at[j, lax.rem(c, q)], o_send.at[j, u], o_recv.at[j],
                lax.div(c, q), r + R * u,
            )

    diag_sub = lax.broadcasted_iota(jnp.int32, (LANES, LANES), 0)
    diag_lane = lax.broadcasted_iota(jnp.int32, (LANES, LANES), 1)

    def times(chunk, s):
        total = None
        for t in range(m):
            term = chunk[:, t * LANES : (t + 1) * LANES] * xs[t // G, t % G : t % G + 1, :]
            total = term if total is None else total + term
        acc[s] = total

    def multiply_groups(j, low, high):
        @pl.loop(low, high)
        def _(g):
            cuts = [rp * u // max(sp, 1) for u in range(max(sp, 1) + 1)]
            for u in range(max(sp, 1)):
                @pl.loop(cuts[u], cuts[u + 1])
                def _(i):
                    if j == 0:
                        res_copy(g, i).wait()
                    times(res.at[g * rp + i], i)

                if sp:
                    seq = j * groups * sp + g * sp + u
                    ring_copy(seq).wait()
                    times(ring.at[lax.rem(seq, nring)], rp + u)

                    @pl.when(seq + nring < K * groups * sp)
                    def _():
                        ring_copy(seq + nring).start()

            for s in range(G):
                line = jnp.sum(acc[s], axis=1, keepdims=True)
                line = jnp.where(diag_sub == diag_lane, line, 0.0)
                pbuf[j, g, s : s + 1, :] = jnp.sum(line, axis=0, keepdims=True)
            p_targets(j, g, send)

    zero = jnp.zeros((1, 1), jnp.float32)
    early = groups - max(1, groups // 3)
    v_top, t_cols = [], []
    arrived(av.at[pl.ds(0, 1)], av_sem.at[0])

    for j in range(K):
        if j == 0:
            x = load(av, 0)
        store(xs, [jnp.where(w > j + 1, a, 0.0) for w, a in zip(where_at, x)])
        x_top_row = jnp.where(first_col, x[0][0:1, :], 0.0)
        sbuf[j, 0] = jnp.zeros((8, LANES), jnp.float32)
        sbuf[j, 1] = jnp.zeros((8, LANES), jnp.float32)
        sbuf[j, 0 if j else 1, K + 1 : K + 2, :] = x_top_row

        if j:
            for i in range(j):
                sbuf[j, 0, i : i + 1, :] = dots(load(vs, i), x)
            round_send(j, 0)
            o_targets(j - 1, send)
            multiply_groups(j, 0, early)
            got = round_get(j, 0)
            left = [lane_total(got[i : i + 1, :]) for i in range(j)]
            w = []
            for k in range(j):
                total = zero
                for i in range(k + 1):
                    total = total + t_cols[k][i] * left[i]
                w.append(total)
            b, b_top = x, got[K + 1 : K + 2, :]
            for i in range(j):
                b = less(b, w[i], load(vs, i))
                b_top = b_top - w[i] * v_top[i]
        else:
            b, w = x, []
        b = [jnp.where(at > j + 1, a, 0.0) for at, a in zip(where_at, b)]
        for i in range(j):
            sbuf[j, 1, i : i + 1, :] = dots(load(vs, i), b)
        sbuf[j, 1, K : K + 1, :] = dots(b, b)
        round_send(j, 1)
        multiply_groups(j, early if j else 0, groups)

        got = round_get(j, 1)
        if j == 0:
            b_top = got[K + 1 : K + 2, :]
            arrived(av.at[pl.ds(1, K)], av_sem.at[1])
        squares = lane_total(got[K : K + 1, :])
        pivot = pick(b_top, j + 1)
        length = jnp.sqrt(pivot * pivot + squares)
        beta = -jnp.where(pivot >= 0, 1.0, -1.0) * length
        tau = (beta - pivot) / beta
        div = pivot - beta
        cross = [lane_total(got[i : i + 1, :]) / div + pick(v_top[i], j + 1) for i in range(j)]
        v = [a / div + jnp.where(at == j + 1, 1.0, 0.0) for at, a in zip(where_at, b)]
        store(vs, v, j)
        store(vy, v, j, 1)
        new_top = jnp.where(lane1 > j + 1, b_top / div, 0.0) + jnp.where(lane1 == j + 1, 1.0, 0.0)

        v_top.append(new_top)
        column = []
        for i in range(j):
            total = zero
            for k in range(i, j):
                total = total + t_cols[k][i] * cross[k]
            column.append(-tau * total)
        t_cols.append(column + [tau])

        fix = [jnp.zeros((G, LANES), jnp.float32)] * ng
        for i in range(j):
            fix = less(fix, w[i], load(ps, i))
        for k in range(j + 2 if j else 0):
            back = zero
            for i in range(j):
                back = back - w[i] * pick(v_top[i], k)
            fix = less(fix, back, load(av, k))
        y_fix = load(av, j + 1)
        for i in range(j):
            y_fix = less(y_fix, cross[i], load(ys, i))
        if j + 1 < K:
            x = load(av, j + 1)
            for i in range(j):
                x = less(x, pick(v_top[i], j + 1), load(ys, i))
            entry = pick(new_top, j + 1)

        arrived(rbuf.at[j], p_recv.at[j])
        p = load(rbuf, j, 0)
        for n in range(1, C):
            p = [a + b_ for a, b_ in zip(p, load(rbuf, j, n))]
        p = [(a + e) / div for a, e in zip(p, fix)]
        y = [tau * (a + e) for a, e in zip(p, y_fix)]
        if j + 1 < K:
            x = less(x, entry, y)
        store(vy, y, j, 0)
        store(ys, y, j)
        store(ps, [a + e for a, e in zip(p, load(av, j + 1))], j)
        if j + 1 == K:
            o_targets(j, send)

    ti = lax.broadcasted_iota(jnp.int32, (K, K), 0)
    tj = lax.broadcasted_iota(jnp.int32, (K, K), 1)
    t_all = jnp.zeros((K, K), jnp.float32)
    for j in range(K):
        for i in range(j + 1):
            t_all = jnp.where(jnp.logical_and(ti == i, tj == j), t_cols[j][i], t_all)
    t_ref[...] = t_all

    for j in range(K):
        arrived(ob.at[j], o_recv.at[j])
    o_ref[...] = ob[...]

    @pl.when(c == 0)
    def _():
        panel_sends(sent)

    for j in range(K):
        for k in range(0 if j else 1, 2):
            arrived(rnd.at[j, k, pl.ds(0, C - 1)], s_send.at[j, k])

        @pl.loop(0, groups)
        def _(g):
            p_targets(j, g, sent)

        o_targets(j, sent)


def lay_out(o_ref, t_in, y_ref, v_ref, t_ref):
    _, q, _, ng, G, _ = o_ref.shape
    for h in range(q):
        for n in range(ng):
            for s in range(G):
                at = ((h * ng + n) * G + s) * LANES
                for j in range(K):
                    y_ref[j : j + 1, at : at + LANES] = o_ref[j, h, 0, n, s : s + 1, :]
                    v_ref[j : j + 1, at : at + LANES] = o_ref[j, h, 1, n, s : s + 1, :]
    t_ref[...] = t_in[...]


def solution(mesh):
    R, C = mesh.shape["row"], mesh.shape["col"]

    def on_device(matrix):
        rows, cols = matrix.shape
        q, m, G, ng, groups, ring, sp = plan(R, C, rows, cols)
        f32 = lambda *shape: pltpu.VMEM(shape, jnp.float32)
        dma = lambda *shape: pltpu.SemaphoreType.DMA(shape)
        nres = groups * (G - sp)
        blocks, t_block = pl.pallas_call(
            functools.partial(kernel, R, C),
            out_shape=(
                jax.ShapeDtypeStruct((K, q, 2, ng, G, LANES), jnp.float32),
                jax.ShapeDtypeStruct((K, K), jnp.float32),
            ),
            in_specs=[pl.BlockSpec(memory_space=pl.ANY)],
            out_specs=(pl.BlockSpec(memory_space=pltpu.VMEM),) * 2,
            scratch_shapes=[
                f32(nres, LANES, cols),
                f32(ring, LANES, cols),
                f32(G, LANES, LANES),
                f32(K + 1, groups, G, LANES),
                f32(K + 1, ng, G, LANES),
                f32(ng, G, LANES),
                f32(K, groups, G, LANES),
                f32(K, C, ng, G, LANES),
                f32(K, 2, 8, LANES),
                f32(K, 2, C, 8, LANES),
                f32(K, 2, ng, G, LANES),
                f32(K, q, 2, ng, G, LANES),
                f32(K, ng, G, LANES),
                f32(K, ng, G, LANES),
                f32(K, ng, G, LANES),
                dma(nres),
                dma(ring),
                pltpu.SemaphoreType.DMA,
                dma(2, q, R),
                dma(2),
                dma(K, groups, R),
                dma(K),
                dma(K, 2),
                dma(K, 2),
                dma(K, q),
                dma(K),
            ],
            compiler_params=pltpu.CompilerParams(
                collective_id=0, has_side_effects=True, vmem_limit_bytes=VMEM_BYTES
            ),
        )(matrix)
        return pl.pallas_call(
            lay_out,
            out_shape=(
                jax.ShapeDtypeStruct((K, rows), jnp.float32),
                jax.ShapeDtypeStruct((K, rows), jnp.float32),
                jax.ShapeDtypeStruct((K, K), jnp.float32),
            ),
            in_specs=[pl.BlockSpec(memory_space=pltpu.VMEM)] * 2,
            out_specs=(pl.BlockSpec(memory_space=pltpu.VMEM),) * 3,
        )(blocks, t_block)

    return jax.shard_map(
        on_device,
        mesh=mesh,
        in_specs=(P("row", "col"),),
        out_specs=(P(None, "row"), P(None, "row"), P()),
        check_vma=False,
    )
```

profile of v0, /device:TPU:0, one launch (start us, length us, event | category | flops | bytes accessed | tf_op | source)
XLA Modules:
  0.0 72.7 jit_solution(4346351587690550575)
XLA Ops:
  0.6 70.4 %shard_map.38 = (f32[4,2,2,3,8,128]{5,4,3,2,1,0:T(8,128)}, f32[4,4]{1,0:T(4,128)}) custom-call(f32[6144,3072]{1,0:T(8,128)} %a_hbm.1), custom_call_target="tpu_custom_call" | custom-call | tf_op jit(solution)/shard_map/pallas_call | solution.py:391
  71.0 1.7 %shard_map.39 = (f32[4,6144]{1,0:T(4,128)}, f32[4,6144]{1,0:T(4,128)}, f32[4,4]{1,0:T(4,128)}) custom-call(f32[4,2,2,3,8,128]{5,4,3,2,1,0:T(8,128)} %get-tuple-element.5.o_ref, f32[4,4]{1,0:T(4,128)} %get-tuple-element.6.t_in), custom_call_target="tpu_custom_call" | custom-call | tf_op jit(solution)/shard_map/pallas_call | solution.py:431
where the time goes:
time: 73.3 us; the launch traced here: 72.7 us
  Pallas kernels  72.1 us (98%)
    pallas_call x1, Pallas kernels, on_device(): pl.pallas_call(functools.partial(kernel, R, C), out_shape=(jax.ShapeDtype...  70.4 us
    pallas_call x1, Pallas kernels, on_device(): pl.pallas_call(lay_out, out_shape=(jax.ShapeDtypeStruct((K, rows), jnp.fl...  1.74 us

commit v1 on v0

v1 whole, which is shorter than its diff:
```python
import functools

import jax
import jax.numpy as jnp
from jax import lax
from jax.experimental import pallas as pl
from jax.experimental.pallas import tpu as pltpu
from jax.sharding import PartitionSpec as P

K = 4
LANES = 128
MESH = pl.DeviceIdType.MESH
VMEM_BYTES = 67043328
SPARE_BYTES = 5 * 2**19


def plan(R, C, rows, cols):
    q = C // R
    m = cols // LANES
    G = 8 if m % 8 == 0 else m
    ng = m // G
    groups = q * ng
    room = (VMEM_BYTES - SPARE_BYTES) // (LANES * cols * 4)
    slots = min(groups * G, room) // 2 * 2
    assert 2 * slots >= groups * G and slots >= q and G % 2 == 0 and slots % 2 == 0
    return q, m, G, ng, groups, slots


def lane_total(row):
    return jnp.sum(row, axis=-1, keepdims=True)


def kernel(
    R, C, a_hbm, o_ref, t_ref,
    pool, acc, pan, av, xs, pbuf, rbuf, lbuf, sbuf, rnd, vy, ob, oav, ox, vs, ys, ps, kept, index,
    pool_sem, pan_sem, pan_send, av_sem, p_send, p_recv, s_send, s_recv, o_send, o_recv,
):
    rows, cols = a_hbm.shape
    q, m, G, ng, groups, slots = plan(R, C, rows, cols)
    tiles = groups * G
    spill = tiles - slots
    r = lax.axis_index("row")
    c = lax.axis_index("col")

    def send(src, dst, send_sem, recv_sem, tr, tc):
        same = jnp.logical_and(tr == r, tc == c)

        @pl.when(jnp.logical_not(same))
        def _():
            pltpu.make_async_remote_copy(
                src, dst, send_sem, recv_sem, device_id=(tr, tc), device_id_type=MESH
            ).start()

        @pl.when(same)
        def _():
            pltpu.make_async_copy(src, dst, recv_sem).start()

    def sent(src, dst, send_sem, recv_sem, tr, tc):
        same = jnp.logical_and(tr == r, tc == c)

        @pl.when(jnp.logical_not(same))
        def _():
            pltpu.make_async_remote_copy(
                src, dst, send_sem, recv_sem, device_id=(tr, tc), device_id_type=MESH
            ).wait_send()

    def arrived(ref, sem):
        pltpu.make_async_copy(ref, ref, sem).wait()

    def panel_copy(t):
        return pltpu.make_async_copy(
            a_hbm.at[pl.ds(pl.multiple_of(t * LANES, LANES), LANES), pl.ds(0, LANES)],
            pool.at[
                slots - q + lax.div(t, m), :,
                pl.ds(pl.multiple_of(lax.rem(t, m) * LANES, LANES), LANES),
            ],
            pan_sem,
        )

    @pl.when(c == 0)
    def _():
        @pl.loop(0, q * m)
        def _(t):
            panel_copy(t).start()

    def tile_copy(t):
        slot = lax.rem(t, slots)
        row = pl.multiple_of(t * LANES, LANES)
        return pltpu.make_async_copy(
            a_hbm.at[pl.ds(row, LANES)], pool.at[slot], pool_sem.at[slot]
        )

    @pl.loop(0, slots - q)
    def _(t):
        tile_copy(t).start()

    barrier = pltpu.get_barrier_semaphore()
    me = r * C + c

    @pl.loop(1, R * C)
    def _(k):
        t = lax.rem(me + k, R * C)
        pl.semaphore_signal(
            barrier, inc=1, device_id=(lax.div(t, C), lax.rem(t, C)), device_id_type=MESH
        )

    def panel_sends(act):
        for part in range(2):
            for piece in range(q):
                for tr in range(R):
                    first, count = (0, 1) if part == 0 else (1, K)
                    act(
                        pan.at[pl.ds(first, count), pl.ds(piece * ng, ng)],
                        av.at[pl.ds(first, count)],
                        pan_send.at[part, piece, tr],
                        av_sem.at[part],
                        jnp.int32(tr),
                        r * q + piece,
                    )

    @pl.when(c == 0)
    def _():
        arrived(pool.at[pl.ds(slots - q, q)], pan_sem)

        @pl.loop(0, groups)
        def _(g):
            slot = slots - q + lax.div(g, ng)
            for s in range(G):
                at = pl.multiple_of((lax.rem(g, ng) * G + s) * LANES, LANES)
                turned = pool[slot, :, pl.ds(at, LANES)].T
                for k in range(K + 1):
                    pan[k, g, s : s + 1, :] = turned[k : k + 1, :]

    @pl.loop(slots - q, slots)
    def _(t):
        tile_copy(t).start()

    pl.semaphore_wait(barrier, R * C - 1)

    @pl.when(c == 0)
    def _():
        panel_sends(send)

    sub = lax.broadcasted_iota(jnp.int32, (G, LANES), 0)
    lane = lax.broadcasted_iota(jnp.int32, (G, LANES), 1)
    for n in range(ng):
        index[n] = c * cols + (n * G + sub) * LANES + lane
    for g in range(groups):
        index[ng + g] = r * rows + (g * G + sub) * LANES + lane
    lane1 = lax.broadcasted_iota(jnp.int32, (1, LANES), 1)
    first_col = (jnp.zeros((1, LANES), jnp.int32) + c) == 0

    def load(ref, *at):
        return [ref[(*at, n)] for n in range(ng)]

    def store(ref, value, *at):
        for n in range(ng):
            ref[(*at, n)] = value[n]

    def pick(row, k):
        return lane_total(jnp.where(lane1 == k, row, 0.0))

    def dots(one, two):
        total = one[0] * two[0]
        for n in range(1, ng):
            total = total + one[n] * two[n]
        return jnp.sum(total, axis=0, keepdims=True)

    def less(value, scale, other):
        return [a - scale * b for a, b in zip(value, other)]

    def round_copy(j, k, o):
        tc = lax.rem(c + o, C)
        return pltpu.make_async_remote_copy(
            sbuf.at[j, k], rnd.at[j, k, c], s_send.at[j, k], s_recv.at[j, k],
            device_id=(r, tc), device_id_type=MESH,
        )

    def round_send(j, k):
        rnd[j, k, c] = sbuf[j, k]

        @pl.loop(1, C)
        def _(o):
            round_copy(j, k, o).start()

    def round_get(j, k):
        arrived(rnd.at[j, k, pl.ds(0, C - 1)], s_recv.at[j, k])
        total = rnd[j, k, 0]
        for n in range(1, C):
            total = total + rnd[j, k, n]
        return total

    def places():
        return [index[n] for n in range(ng)]

    def keep(at, value):
        kept[at : at + 1, :] = jnp.broadcast_to(value, (1, LANES))

    def row_of(at):
        return kept[at : at + 1, :]

    def scalar(at):
        return kept[at : at + 1, 0:1]

    def T_AT(i, j):
        return i * K + j

    def CROSS_AT(i, j):
        return K * K + i * K + j

    def TOP_AT(i):
        return 2 * K * K + i

    def p_targets(j, g):
        if j + 1 == K:
            for tc in range(C):
                send(
                    pbuf.at[j, g], lbuf.at[c, g], p_send.at[j], p_recv.at[j], r, jnp.int32(tc)
                )
            return
        piece, part = lax.div(g, ng), lax.rem(g, ng)
        for tr in range(R):
            send(
                pbuf.at[j, g], rbuf.at[j, c, part], p_send.at[j], p_recv.at[j],
                jnp.int32(tr), r * q + piece,
            )

    def p_sent(j):
        if j + 1 == K:
            arrived(lbuf.at[pl.ds(0, C - 1)], p_send.at[j])
            return
        own = lax.div(c, q) == r

        @pl.when(own)
        def _():
            arrived(rbuf.at[j, pl.ds(0, C - 1)], p_send.at[j])

        @pl.when(jnp.logical_not(own))
        def _():
            arrived(rbuf.at[j], p_send.at[j])

    def o_targets(src, dst, k):
        for u in range(q):
            send(
                src, dst.at[lax.rem(c, q)], o_send.at[k], o_recv.at[k], lax.div(c, q), r + R * u
            )

    def o_sent(dst, k):
        own = jnp.logical_and(lax.div(c, q) == r, lax.rem(c, R) == r)

        @pl.when(own)
        def _():
            arrived(dst.at[pl.ds(0, q - 1)], o_send.at[k])

        @pl.when(jnp.logical_not(own))
        def _():
            arrived(dst, o_send.at[k])

    def r_sent(j, k):
        arrived(rnd.at[j, k, pl.ds(0, C - 1)], s_send.at[j, k])

    def line(j, tile, slot):
        pbuf[j, lax.div(tile, G), pl.ds(lax.rem(tile, G), 1), :] = jnp.sum(
            acc[slot].T, axis=0, keepdims=True
        )

    def multiply(j):
        back = j % 2 == 1
        xb = [
            jnp.broadcast_to(xs[t // G, t % G : t % G + 1, :], (8, LANES)) for t in range(m)
        ]

        def tile_at(at):
            return tiles - 1 - at if back else at

        def finish(at):
            for w in range(2):
                line(j, tile_at(at + w), lax.rem(lax.div(at, 2), 2) * 2 + w)

        @pl.loop(0, tiles // 2)
        def _(pair):
            at = pair * 2
            @pl.loop(jnp.maximum(at, slots) if j else at, at + 2)
            def _(k):
                tile_copy(tile_at(k)).wait()

            finish(jnp.maximum(at - 2, 0))
            for w in range(2):
                slot = lax.rem(tile_at(at + w), slots)
                for u in range(0, LANES, 8):
                    total = None
                    for t in range(m):
                        term = pool[slot, u : u + 8, t * LANES : (t + 1) * LANES] * xb[t]
                        total = term if total is None else total + term
                    acc[lax.rem(pair, 2) * 2 + w, u : u + 8, :] = total

            @pl.loop(at, jnp.minimum(at + 2, spill))
            def _(k):
                tile_copy(tile_at(slots + k)).start()

            full = jnp.logical_and(at > 0, lax.rem(at, G) == 0)

            @pl.loop(0, full.astype(jnp.int32))
            def _(k):
                p_targets(j, lax.div(tile_at(at - 1), G))

        finish(jnp.int32(tiles - 2))
        p_targets(j, jnp.int32(0 if back else groups - 1))

    for w in range(2):
        acc[w] = jnp.zeros((LANES, LANES), jnp.float32)
    zero = jnp.zeros((1, 1), jnp.float32)
    arrived(av.at[pl.ds(0, 1)], av_sem.at[0])

    for j in range(K):
        if j == 0:
            x = load(av, 0)
        store(xs, [jnp.where(w > j + 1, a, 0.0) for w, a in zip(places(), x)])
        x_top_row = jnp.where(first_col, x[0][0:1, :], 0.0)
        sbuf[j, 0] = jnp.zeros((8, LANES), jnp.float32)
        sbuf[j, 1] = jnp.zeros((8, LANES), jnp.float32)
        sbuf[j, 0 if j else 1, K + 1 : K + 2, :] = x_top_row

        if j:
            for i in range(j):
                sbuf[j, 0, i : i + 1, :] = dots(load(vs, i), x)
            round_send(j, 0)
            o_targets(vy.at[j - 1], ob.at[j - 1], j - 1)
            if j == 1:
                o_targets(av, oav, K)
            if j + 1 == K:
                o_targets(xs, ox, j)
        else:
            b = load(xs)
            sbuf[j, 1, K : K + 1, :] = dots(b, b)
            round_send(j, 1)
        multiply(j)

        if j:
            got = round_get(j, 0)
            left = [lane_total(got[i : i + 1, :]) for i in range(j)]
            w = []
            for k in range(j):
                total = zero
                for i in range(k + 1):
                    total = total + scalar(T_AT(i, k)) * left[i]
                w.append(total)
            b, b_top = load(xs), got[K + 1 : K + 2, :]
            for i in range(j):
                b = less(b, w[i], load(vs, i))
                b_top = b_top - w[i] * row_of(TOP_AT(i))
            b = [jnp.where(at > j + 1, a, 0.0) for at, a in zip(places(), b)]
            for i in range(j):
                sbuf[j, 1, i : i + 1, :] = dots(load(vs, i), b)
            sbuf[j, 1, K : K + 1, :] = dots(b, b)
            round_send(j, 1)
            p_sent(j - 1)
            r_sent(j - 1, 1)
            if j > 1:
                o_sent(ob.at[j - 2], j - 2)
                r_sent(j - 1, 0)
        else:
            w = []

            @pl.when(c == 0)
            def _():
                panel_sends(sent)

        got = round_get(j, 1)
        if j == 0:
            b_top = got[K + 1 : K + 2, :]
            arrived(av.at[pl.ds(1, K)], av_sem.at[1])
        v_top = [row_of(TOP_AT(i)) for i in range(j)]
        squares = lane_total(got[K : K + 1, :])
        pivot = pick(b_top, j + 1)
        length = jnp.sqrt(pivot * pivot + squares)
        beta = -jnp.where(pivot >= 0, 1.0, -1.0) * length
        tau = (beta - pivot) / beta
        div = pivot - beta
        cross = [lane_total(got[i : i + 1, :]) / div + pick(v_top[i], j + 1) for i in range(j)]
        new_top = jnp.where(lane1 > j + 1, b_top / div, 0.0) + jnp.where(lane1 == j + 1, 1.0, 0.0)
        keep(TOP_AT(j), new_top)
        for i in range(j):
            total = zero
            for k in range(i, j):
                total = total + scalar(T_AT(i, k)) * cross[k]
            keep(T_AT(i, j), -tau * total)
            keep(CROSS_AT(i, j), cross[i])
        keep(T_AT(j, j), tau)
        back = []
        for k in range(j + 2 if j else 0):
            total = zero
            for i in range(j):
                total = total + w[i] * pick(v_top[i], k)
            back.append(total)

        if j + 1 == K:
            break

        v = [a / div + jnp.where(at == j + 1, 1.0, 0.0) for at, a in zip(places(), b)]
        store(vs, v, j)
        store(vy, v, j, 1)
        fix = [jnp.zeros((G, LANES), jnp.float32)] * ng
        for i in range(j):
            fix = less(fix, w[i], load(ps, i))
        for k, value in enumerate(back):
            fix = less(fix, -value, load(av, k))
        y_fix = load(av, j + 1)
        for i in range(j):
            y_fix = less(y_fix, cross[i], load(ys, i))
        x = load(av, j + 1)
        for i in range(j):
            x = less(x, pick(v_top[i], j + 1), load(ys, i))
        entry = pick(new_top, j + 1)

        arrived(rbuf.at[j], p_recv.at[j])
        p = load(rbuf, j, 0)
        for n in range(1, C):
            p = [a + b_ for a, b_ in zip(p, load(rbuf, j, n))]
        p = [(a + e) / div for a, e in zip(p, fix)]
        y = [tau * (a + e) for a, e in zip(p, y_fix)]
        x = less(x, entry, y)
        store(vy, y, j, 0)
        store(ys, y, j)
        store(ps, [a + e for a, e in zip(p, load(av, j + 1))], j)

    scale = tau / div
    y_part, a_part = [], []
    for i in range(K - 1):
        total = w[i] / scalar(T_AT(i, i))
        for k in range(i + 1, K - 1):
            total = total + w[k] * scalar(CROSS_AT(i, k))
        y_part.append(-tau * (total / div + cross[i]))
    for k in range(K + 1):
        a_part.append(scale * back[k] + (tau if k == K else 0.0))
    for j in range(K - 1):
        arrived(ob.at[j], o_recv.at[j])
    arrived(ox, o_recv.at[K - 1])
    arrived(oav, o_recv.at[K])
    for g in range(groups):
        h, n = g // ng, g % ng
        at = index[ng + g]
        b = ox[h, n]
        rest = a_part[0] * oav[h, 0, n]
        for k in range(1, K + 1):
            rest = rest + a_part[k] * oav[h, k, n]
        for i in range(K - 1):
            y, v = ob[i, h, 0, n], ob[i, h, 1, n]
            o_ref[i, h, 0, n] = y
            o_ref[i, h, 1, n] = v
            b = b - w[i] * v
            rest = rest + y_part[i] * y
        v = jnp.where(at > K, b, 0.0) / div + jnp.where(at == K, 1.0, 0.0)
        o_ref[K - 1, h, 1, n] = v
        o_ref[K - 1, h, 0, n] = rest

    ti = lax.broadcasted_iota(jnp.int32, (K, K), 0)
    tj = lax.broadcasted_iota(jnp.int32, (K, K), 1)
    t_all = jnp.zeros((K, K), jnp.float32)
    for j in range(K):
        for i in range(j + 1):
            t_all = jnp.where(jnp.logical_and(ti == i, tj == j), scalar(T_AT(i, j)), t_all)
    t_ref[...] = t_all

    r_sent(K - 1, 0)
    r_sent(K - 1, 1)
    o_sent(ob.at[K - 2], K - 2)
    o_sent(ox, K - 1)
    o_sent(oav, K)
    arrived(lbuf, p_recv.at[K - 1])
    for g in range(groups):
        total = lbuf[0, g]
        for n in range(1, C):
            total = total + lbuf[n, g]
        h, n = g // ng, g % ng
        o_ref[K - 1, h, 0, n] = scale * total + o_ref[K - 1, h, 0, n]
    p_sent(K - 1)


def lay_out(o_ref, t_in, y_ref, v_ref, t_ref):
    _, q, _, ng, G, _ = o_ref.shape
    for h in range(q):
        for n in range(ng):
            for s in range(G):
                at = ((h * ng + n) * G + s) * LANES
                for j in range(K):
                    y_ref[j : j + 1, at : at + LANES] = o_ref[j, h, 0, n, s : s + 1, :]
                    v_ref[j : j + 1, at : at + LANES] = o_ref[j, h, 1, n, s : s + 1, :]
    t_ref[...] = t_in[...]


def solution(mesh):
    R, C = mesh.shape["row"], mesh.shape["col"]

    def on_device(matrix):
        rows, cols = matrix.shape
        q, m, G, ng, groups, slots = plan(R, C, rows, cols)
        f32 = lambda *shape: pltpu.VMEM(shape, jnp.float32)
        dma = lambda *shape: pltpu.SemaphoreType.DMA(shape)
        blocks, t_block = pl.pallas_call(
            functools.partial(kernel, R, C),
            out_shape=(
                jax.ShapeDtypeStruct((K, q, 2, ng, G, LANES), jnp.float32),
                jax.ShapeDtypeStruct((K, K), jnp.float32),
            ),
            in_specs=[pl.BlockSpec(memory_space=pl.ANY)],
            out_specs=(pl.BlockSpec(memory_space=pltpu.VMEM),) * 2,
            scratch_shapes=[
                f32(slots, LANES, cols),
                f32(4, LANES, LANES),
                f32(K + 1, groups, G, LANES),
                f32(K + 1, ng, G, LANES),
                f32(ng, G, LANES),
                f32(K, groups, G, LANES),
                f32(K - 1, C, ng, G, LANES),
                f32(C, groups, G, LANES),
                f32(K, 2, 8, LANES),
                f32(K, 2, C, 8, LANES),
                f32(K - 1, 2, ng, G, LANES),
                f32(K - 1, q, 2, ng, G, LANES),
                f32(q, K + 1, ng, G, LANES),
                f32(q, ng, G, LANES),
                f32(K - 1, ng, G, LANES),
                f32(K - 1, ng, G, LANES),
                f32(K - 1, ng, G, LANES),
                f32(2 * K * K + K, LANES),
                pltpu.VMEM((ng + groups, G, LANES), jnp.int32),
                dma(slots),
                pltpu.SemaphoreType.DMA,
                dma(2, q, R),
                dma(2),
                dma(K),
                dma(K),
                dma(K, 2),
                dma(K, 2),
                dma(K + 1),
                dma(K + 1),
            ],
            compiler_params=pltpu.CompilerParams(
                collective_id=0, has_side_effects=True, vmem_limit_bytes=VMEM_BYTES,

            ),
        )(matrix)
        return pl.pallas_call(
            lay_out,
            out_shape=(
                jax.ShapeDtypeStruct((K, rows), jnp.float32),
                jax.ShapeDtypeStruct((K, rows), jnp.float32),
                jax.ShapeDtypeStruct((K, K), jnp.float32),
            ),
            in_specs=[pl.BlockSpec(memory_space=pltpu.VMEM)] * 2,
            out_specs=(pl.BlockSpec(memory_space=pltpu.VMEM),) * 3,
        )(blocks, t_block)

    return jax.shard_map(
        on_device,
        mesh=mesh,
        in_specs=(P("row", "col"),),
        out_specs=(P(None, "row"), P(None, "row"), P()),
        check_vma=False,
    )
```

time: 73.3 us -> 69.7 us (0.951)
  Pallas kernels: 72.1 us -> 68.9 us
    pallas_call x1, Pallas kernels: 70.4 us -> 67.1 us  [on_device(): pl.pallas_call(functools.partial(kernel, R, C), out_shape=(jax.ShapeDtype...]
where the time goes in v1:
time: 69.7 us; the launch traced here: 69.5 us
  Pallas kernels  68.9 us (99%)
    pallas_call x1, Pallas kernels, on_device(): pl.pallas_call(functools.partial(kernel, R, C), out_shape=(jax.ShapeDtype...  67.1 us
    pallas_call x1, Pallas kernels, on_device(): pl.pallas_call(lay_out, out_shape=(jax.ShapeDtypeStruct((K, rows), jnp.fl...  1.74 us

profile of v1, /device:TPU:0, one launch (start us, length us, event | category | flops | bytes accessed | tf_op | source)
XLA Modules:
  0.0 69.5 jit_solution(8632859325649706024)
XLA Ops:
  0.6 67.1 %shard_map.38 = (f32[4,2,2,3,8,128]{5,4,3,2,1,0:T(8,128)}, f32[4,4]{1,0:T(4,128)}) custom-call(f32[6144,3072]{1,0:T(8,128)} %a_hbm.1), custom_call_target="tpu_custom_call" | custom-call | tf_op jit(solution)/shard_map/pallas_call | solution.py:500
  67.8 1.7 %shard_map.39 = (f32[4,6144]{1,0:T(4,128)}, f32[4,6144]{1,0:T(4,128)}, f32[4,4]{1,0:T(4,128)}) custom-call(f32[4,2,2,3,8,128]{5,4,3,2,1,0:T(8,128)} %get-tuple-element.5.o_ref, f32[4,4]{1,0:T(4,128)} %get-tuple-element.6.t_in), custom_call_target="tpu_custom_call" | custom-call | tf_op jit(solution)/shard_map/pallas_call | solution.py:544

commit v2 on v1

--- a/solution.py
+++ b/solution.py
@@ -32,7 +32,7 @@
 
 def kernel(
     R, C, a_hbm, o_ref, t_ref,
-    pool, acc, pan, av, xs, pbuf, rbuf, lbuf, sbuf, rnd, vy, ob, oav, ox, vs, ys, ps, kept, index,
+    pool, acc, pan, av, xs, pbuf, rbuf, lbuf, sbuf, rnd, vy, ob, oav, ox, vs, ys, ps, bs, kept, index,
     pool_sem, pan_sem, pan_send, av_sem, p_send, p_recv, s_send, s_recv, o_send, o_recv,
 ):
     rows, cols = a_hbm.shape
@@ -211,19 +211,30 @@
     def TOP_AT(i):
         return 2 * K * K + i
 
-    def p_targets(j, g):
+    def push(src, dst, send_sem, recv_sem, tr, tc):
+        pltpu.make_async_remote_copy(
+            src, dst, send_sem, recv_sem, device_id=(tr, tc), device_id_type=MESH
+        ).start()
+
+    def W_AT(i):
+        return 2 * K * K + K + i
+
+    def p_targets(j, g, count=1):
+        block = pbuf.at[j, pl.ds(g, count)]
         if j + 1 == K:
-            for tc in range(C):
-                send(
-                    pbuf.at[j, g], lbuf.at[c, g], p_send.at[j], p_recv.at[j], r, jnp.int32(tc)
+            for o in range(1, C):
+                push(
+                    block, lbuf.at[c, pl.ds(g, count)], p_send.at[j], p_recv.at[j], r,
+                    lax.rem(c + o, C),
                 )
+            for n in range(count):
+                lbuf[c, g + n] = pbuf[j, g + n]
             return
         piece, part = lax.div(g, ng), lax.rem(g, ng)
-        for tr in range(R):
-            send(
-                pbuf.at[j, g], rbuf.at[j, c, part], p_send.at[j], p_recv.at[j],
-                jnp.int32(tr), r * q + piece,
-            )
+        there, tc = rbuf.at[j, c, pl.ds(part, count)], r * q + piece
+        for o in range(1, R):
+            push(block, there, p_send.at[j], p_recv.at[j], lax.rem(r + o, R), tc)
+        send(block, there, p_send.at[j], p_recv.at[j], r, tc)
 
     def p_sent(j):
         if j + 1 == K:
@@ -264,11 +275,8 @@
             acc[slot].T, axis=0, keepdims=True
         )
 
-    def multiply(j):
+    def multiply(j, late):
         back = j % 2 == 1
-        xb = [
-            jnp.broadcast_to(xs[t // G, t % G : t % G + 1, :], (8, LANES)) for t in range(m)
-        ]
 
         def tile_at(at):
             return tiles - 1 - at if back else at
@@ -277,37 +285,69 @@
             for w in range(2):
                 line(j, tile_at(at + w), lax.rem(lax.div(at, 2), 2) * 2 + w)
 
-        @pl.loop(0, tiles // 2)
-        def _(pair):
-            at = pair * 2
-            @pl.loop(jnp.maximum(at, slots) if j else at, at + 2)
+        def pairs(low, count, done):
+            xb = [
+                jnp.broadcast_to(xs[t // G, t % G : t % G + 1, :], (8, LANES))
+                for t in range(m)
+            ]
+
+            @pl.loop(0, count // 2)
+            def _(pair):
+                at = low + pair * 2
+                if j == 0:
+                    for w in range(2):
+                        tile_copy(tile_at(at + w)).wait()
+                half = lax.rem(lax.div(at, 2), 2) * 2
+                for w in range(2):
+                    line(j, tile_at(jnp.maximum(at - 2, done) + w), 2 - half + w)
+                for w in range(2):
+                    slot = lax.rem(tile_at(at + w), slots)
+                    for u in range(0, LANES, 8):
+                        total = None
+                        for t in range(m):
+                            term = pool[slot, u : u + 8, t * LANES : (t + 1) * LANES] * xb[t]
+                            total = term if total is None else total + term
+                        acc[half + w, u : u + 8, :] = total
+
+        if j == 0:
+            @pl.loop(0, groups)
             def _(k):
-                tile_copy(tile_at(k)).wait()
-
-            finish(jnp.maximum(at - 2, 0))
-            for w in range(2):
-                slot = lax.rem(tile_at(at + w), slots)
-                for u in range(0, LANES, 8):
-                    total = None
-                    for t in range(m):
-                        term = pool[slot, u : u + 8, t * LANES : (t + 1) * LANES] * xb[t]
-                        total = term if total is None else total + term
-                    acc[lax.rem(pair, 2) * 2 + w, u : u + 8, :] = total
-
-            @pl.loop(at, jnp.minimum(at + 2, spill))
-            def _(k):
-                tile_copy(tile_at(slots + k)).start()
-
-            full = jnp.logical_and(at > 0, lax.rem(at, G) == 0)
-
-            @pl.loop(0, full.astype(jnp.int32))
-            def _(k):
-                p_targets(j, lax.div(tile_at(at - 1), G))
-
-        finish(jnp.int32(tiles - 2))
-        p_targets(j, jnp.int32(0 if back else groups - 1))
-
-    for w in range(2):
+                start = k * G
+                pairs(start, G, start)
+                finish(start + G - 2)
+                p_targets(j, lax.div(tile_at(start), G))
+
+                @pl.loop(start, jnp.minimum(start + G, spill))
+                def _(at):
+                    tile_copy(tile_at(slots + at)).start()
+            return
+
+        ends = [k * ng for k in range(1, q + 1)]
+        if ng > 1:
+            ends.append(groups - 1)
+        cuts = sorted({0, *ends, min(groups, pl.cdiv(spill, G)), slots // G})
+        sent_to = 0
+        for low, high in zip(cuts, cuts[1:]):
+            if low == cuts[-2]:
+                late()
+
+            if high * G > slots:
+                @pl.loop(max(low * G, slots), high * G)
+                def _(at):
+                    tile_copy(tile_at(at)).wait()
+
+            pairs(low * G, (high - low) * G, sent_to * G)
+            if high in ends:
+                finish(jnp.int32(high * G - 2))
+                first = groups - high if back else sent_to
+                p_targets(j, jnp.int32(first), high - sent_to)
+                sent_to = high
+            if low * G < spill:
+                @pl.loop(low * G, min(high * G, spill))
+                def _(at):
+                    tile_copy(tile_at(slots + at)).start()
+
+    for w in range(4):
         acc[w] = jnp.zeros((LANES, LANES), jnp.float32)
     zero = jnp.zeros((1, 1), jnp.float32)
     arrived(av.at[pl.ds(0, 1)], av_sem.at[0])
@@ -325,7 +365,8 @@
             for i in range(j):
                 sbuf[j, 0, i : i + 1, :] = dots(load(vs, i), x)
             round_send(j, 0)
-            o_targets(vy.at[j - 1], ob.at[j - 1], j - 1)
+            if j + 1 == K:
+                o_targets(vy.at[j - 1], ob.at[j - 1], j - 1)
             if j == 1:
                 o_targets(av, oav, K)
             if j + 1 == K:
@@ -334,26 +375,32 @@
             b = load(xs)
             sbuf[j, 1, K : K + 1, :] = dots(b, b)
             round_send(j, 1)
-        multiply(j)
-
-        if j:
+        def second_round():
             got = round_get(j, 0)
             left = [lane_total(got[i : i + 1, :]) for i in range(j)]
-            w = []
+            b, b_top = load(xs), got[K + 1 : K + 2, :]
             for k in range(j):
                 total = zero
                 for i in range(k + 1):
                     total = total + scalar(T_AT(i, k)) * left[i]
-                w.append(total)
-            b, b_top = load(xs), got[K + 1 : K + 2, :]
-            for i in range(j):
-                b = less(b, w[i], load(vs, i))
-                b_top = b_top - w[i] * row_of(TOP_AT(i))
+                keep(W_AT(k), total)
+                b = less(b, total, load(vs, k))
+                b_top = b_top - total * row_of(TOP_AT(k))
+            keep(W_AT(K), b_top)
             b = [jnp.where(at > j + 1, a, 0.0) for at, a in zip(places(), b)]
+            store(bs, b)
             for i in range(j):
                 sbuf[j, 1, i : i + 1, :] = dots(load(vs, i), b)
             sbuf[j, 1, K : K + 1, :] = dots(b, b)
             round_send(j, 1)
+
+        multiply(j, second_round)
+
+        if j:
+            w = [scalar(W_AT(i)) for i in range(j)]
+            b, b_top = load(bs), row_of(W_AT(K))
+            if j + 1 < K:
+                o_targets(vy.at[j - 1], ob.at[j - 1], j - 1)
             p_sent(j - 1)
             r_sent(j - 1, 1)
             if j > 1:
@@ -467,7 +514,7 @@
     o_sent(ob.at[K - 2], K - 2)
     o_sent(ox, K - 1)
     o_sent(oav, K)
-    arrived(lbuf, p_recv.at[K - 1])
+    arrived(lbuf.at[pl.ds(0, C - 1)], p_recv.at[K - 1])
     for g in range(groups):
         total = lbuf[0, g]
         for n in range(1, C):
@@ -523,7 +570,8 @@
                 f32(K - 1, ng, G, LANES),
                 f32(K - 1, ng, G, LANES),
                 f32(K - 1, ng, G, LANES),
-                f32(2 * K * K + K, LANES),
+                f32(ng, G, LANES),
+                f32(2 * K * K + 2 * K + 1, LANES),
                 pltpu.VMEM((ng + groups, G, LANES), jnp.int32),
                 dma(slots),
                 pltpu.SemaphoreType.DMA,

time: 69.7 us -> 67.7 us (0.971)
  Pallas kernels: 68.9 us -> 66.9 us
    pallas_call x1, Pallas kernels: 67.1 us -> 65.1 us  [on_device(): pl.pallas_call(functools.partial(kernel, R, C), out_shape=(jax.ShapeDtype...]
where the time goes in v2:
time: 67.7 us; the launch traced here: 67.5 us
  Pallas kernels  66.9 us (99%)
    pallas_call x1, Pallas kernels, on_device(): pl.pallas_call(functools.partial(kernel, R, C), out_shape=(jax.ShapeDtype...  65.1 us
    pallas_call x1, Pallas kernels, on_device(): pl.pallas_call(lay_out, out_shape=(jax.ShapeDtypeStruct((K, rows), jnp.fl...  1.74 us

profile of v2, /device:TPU:0, one launch (start us, length us, event | category | flops | bytes accessed | tf_op | source)
XLA Modules:
  0.0 67.5 jit_solution(5660813491917787598)
XLA Ops:
  0.6 65.1 %shard_map.38 = (f32[4,2,2,3,8,128]{5,4,3,2,1,0:T(8,128)}, f32[4,4]{1,0:T(4,128)}) custom-call(f32[6144,3072]{1,0:T(8,128)} %a_hbm.1), custom_call_target="tpu_custom_call" | custom-call | tf_op jit(solution)/shard_map/pallas_call | solution.py:547
  65.8 1.7 %shard_map.39 = (f32[4,6144]{1,0:T(4,128)}, f32[4,6144]{1,0:T(4,128)}, f32[4,4]{1,0:T(4,128)}) custom-call(f32[4,2,2,3,8,128]{5,4,3,2,1,0:T(8,128)} %get-tuple-element.5.o_ref, f32[4,4]{1,0:T(4,128)} %get-tuple-element.6.t_in), custom_call_target="tpu_custom_call" | custom-call | tf_op jit(solution)/shard_map/pallas_call | solution.py:592

commit v3 on v2

--- a/solution.py
+++ b/solution.py
@@ -310,8 +310,7 @@
                         acc[half + w, u : u + 8, :] = total
 
         if j == 0:
-            @pl.loop(0, groups)
-            def _(k):
+            def one(k):
                 start = k * G
                 pairs(start, G, start)
                 finish(start + G - 2)
@@ -320,17 +319,20 @@
                 @pl.loop(start, jnp.minimum(start + G, spill))
                 def _(at):
                     tile_copy(tile_at(slots + at)).start()
+
+            middle = groups // 2 + 1
+            pl.loop(0, middle)(one)
+            late()
+            pl.loop(middle, groups)(one)
             return
 
         ends = [k * ng for k in range(1, q + 1)]
         if ng > 1:
-            ends.append(groups - 1)
+            ends += range(groups - ng + 1, groups)
+        assert groups > 1
         cuts = sorted({0, *ends, min(groups, pl.cdiv(spill, G)), slots // G})
         sent_to = 0
         for low, high in zip(cuts, cuts[1:]):
-            if low == cuts[-2]:
-                late()
-
             if high * G > slots:
                 @pl.loop(max(low * G, slots), high * G)
                 def _(at):
@@ -339,6 +341,8 @@
             pairs(low * G, (high - low) * G, sent_to * G)
             if high in ends:
                 finish(jnp.int32(high * G - 2))
+                if high == cuts[-2]:
+                    late()
                 first = groups - high if back else sent_to
                 p_targets(j, jnp.int32(first), high - sent_to)
                 sent_to = high
@@ -367,8 +371,6 @@
             round_send(j, 0)
             if j + 1 == K:
                 o_targets(vy.at[j - 1], ob.at[j - 1], j - 1)
-            if j == 1:
-                o_targets(av, oav, K)
             if j + 1 == K:
                 o_targets(xs, ox, j)
         else:
@@ -376,6 +378,10 @@
             sbuf[j, 1, K : K + 1, :] = dots(b, b)
             round_send(j, 1)
         def second_round():
+            if j == 0:
+                arrived(av.at[pl.ds(1, K)], av_sem.at[1])
+                o_targets(av, oav, K)
+                return
             got = round_get(j, 0)
             left = [lane_total(got[i : i + 1, :]) for i in range(j)]
             b, b_top = load(xs), got[K + 1 : K + 2, :]
@@ -416,7 +422,6 @@
         got = round_get(j, 1)
         if j == 0:
             b_top = got[K + 1 : K + 2, :]
-            arrived(av.at[pl.ds(1, K)], av_sem.at[1])
         v_top = [row_of(TOP_AT(i)) for i in range(j)]
         squares = lane_total(got[K : K + 1, :])
         pivot = pick(b_top, j + 1)

time: 67.7 us -> 67.5 us (level)
  no operation moved by 1% of the time
where the time goes in v3:
time: 67.5 us; the launch traced here: 67.3 us
  Pallas kernels  66.7 us (99%)
    pallas_call x1, Pallas kernels, on_device(): pl.pallas_call(functools.partial(kernel, R, C), out_shape=(jax.ShapeDtype...  65 us
    pallas_call x1, Pallas kernels, on_device(): pl.pallas_call(lay_out, out_shape=(jax.ShapeDtypeStruct((K, rows), jnp.fl...  1.74 us

profile of v3, /device:TPU:0, one launch (start us, length us, event | category | flops | bytes accessed | tf_op | source)
XLA Modules:
  0.0 67.3 jit_solution(334491811998044943)
XLA Ops:
  0.6 65.0 %shard_map.38 = (f32[4,2,2,3,8,128]{5,4,3,2,1,0:T(8,128)}, f32[4,4]{1,0:T(4,128)}) custom-call(f32[6144,3072]{1,0:T(8,128)} %a_hbm.1), custom_call_target="tpu_custom_call" | custom-call | tf_op jit(solution)/shard_map/pallas_call | solution.py:552
  65.6 1.7 %shard_map.39 = (f32[4,6144]{1,0:T(4,128)}, f32[4,6144]{1,0:T(4,128)}, f32[4,4]{1,0:T(4,128)}) custom-call(f32[4,2,2,3,8,128]{5,4,3,2,1,0:T(8,128)} %get-tuple-element.5.o_ref, f32[4,4]{1,0:T(4,128)} %get-tuple-element.6.t_in), custom_call_target="tpu_custom_call" | custom-call | tf_op jit(solution)/shard_map/pallas_call | solution.py:597

commit v4 on v3

--- a/solution.py
+++ b/solution.py
@@ -339,6 +339,9 @@
                     tile_copy(tile_at(at)).wait()
 
             pairs(low * G, (high - low) * G, sent_to * G)
+            if low == 0 and j + 1 == K:
+                o_targets(xs, ox, j)
+                o_targets(vy.at[j - 1], ob.at[j - 1], j - 1)
             if high in ends:
                 finish(jnp.int32(high * G - 2))
                 if high == cuts[-2]:
@@ -369,10 +372,6 @@
             for i in range(j):
                 sbuf[j, 0, i : i + 1, :] = dots(load(vs, i), x)
             round_send(j, 0)
-            if j + 1 == K:
-                o_targets(vy.at[j - 1], ob.at[j - 1], j - 1)
-            if j + 1 == K:
-                o_targets(xs, ox, j)
         else:
             b = load(xs)
             sbuf[j, 1, K : K + 1, :] = dots(b, b)

time: 67.5 us -> 67.5 us (level)
  no operation moved by 1% of the time
where the time goes in v4:
time: 67.5 us; the launch traced here: 67.3 us
  Pallas kernels  66.7 us (99%)
    pallas_call x1, Pallas kernels, on_device(): pl.pallas_call(functools.partial(kernel, R, C), out_shape=(jax.ShapeDtype...  65 us
    pallas_call x1, Pallas kernels, on_device(): pl.pallas_call(lay_out, out_shape=(jax.ShapeDtypeStruct((K, rows), jnp.fl...  1.74 us

profile of v4, /device:TPU:0, one launch (start us, length us, event | category | flops | bytes accessed | tf_op | source)
XLA Modules:
  0.0 67.3 jit_solution(6643594458306019559)
XLA Ops:
  0.6 65.0 %shard_map.38 = (f32[4,2,2,3,8,128]{5,4,3,2,1,0:T(8,128)}, f32[4,4]{1,0:T(4,128)}) custom-call(f32[6144,3072]{1,0:T(8,128)} %a_hbm.1), custom_call_target="tpu_custom_call" | custom-call | tf_op jit(solution)/shard_map/pallas_call | solution.py:551
  65.6 1.7 %shard_map.39 = (f32[4,6144]{1,0:T(4,128)}, f32[4,6144]{1,0:T(4,128)}, f32[4,4]{1,0:T(4,128)}) custom-call(f32[4,2,2,3,8,128]{5,4,3,2,1,0:T(8,128)} %get-tuple-element.5.o_ref, f32[4,4]{1,0:T(4,128)} %get-tuple-element.6.t_in), custom_call_target="tpu_custom_call" | custom-call | tf_op jit(solution)/shard_map/pallas_call | solution.py:596
